TPU v7x, 256 devices: a whole 4x4x8 slice. The times are simulated.
256 devices in a mesh: grp: 16 (over y, x), seq: 16 (over z, core).
Axes of the slice: x: 4, y: 4, z: 8, core: 2. Of those that a mesh axis runs over, the one named last changes fastest.
Arguments:
- audio: bfloat16 [16, 4096, 1280], P('grp', 'seq'), may hold values from -6 to 6, as said below
- block_ids: int32 [16, 4096], P('grp', 'seq'), may hold values from 0 to 80, never falling along the last dimension, each value on 1 to 100 neighbouring positions
- norm_gain: float32 [1280], replicated, may hold values from 0.1 to 1.9
- qkv_weight: bfloat16 [1280, 3840], P(None, 'grp'), may hold values from -8 to 8
- out_weight: bfloat16 [1280, 1280], P(None, 'grp'), may hold values from -0.15625 to 0.15625
- adapter_weight: bfloat16 [2560, 2048], P(None, 'grp'), may hold values from -0.125 to 0.125
- moe_gain: float32 [2048], replicated, may hold values from 0.1 to 1.9
- gate_weight: bfloat16 [16, 2048, 768], P('seq'), may hold values from -0.125 to 0.125
- up_weight: bfloat16 [16, 2048, 768], P('seq'), may hold values from -0.125 to 0.125
- down_weight: bfloat16 [16, 768, 2048], P('seq'), may hold values from -0.21875 to 0.21875
- routes: int32 [16, 2048, 4], P('grp', 'seq'), may hold values from 0 to 15, all different within a row; in each aligned block of 128 rows (0 to 127, 128 to 255, ..., all dimensions but the last counted through in order) at most 48 rows name the same one
- route_weights: float32 [16, 2048, 4], P('grp', 'seq'), may hold values from 0.05 to 1
Outputs:
- thinker_out: bfloat16 [16, 2048, 2048], P('grp', 'seq')
Inputs may be any that keep to these rules, and one draw needn't show every extreme that they name: `audio`: in the hidden draw, frames come in nearly equal adjacent pairs. `block_ids`: block numbers never fall along a slab's frames; each block holds 1 to 100 frames, and some block exactly 100. `routes`: each token names 4 different experts; among the tokens of one device no expert is named by more than 48 of them, and in every draw some expert is named by exactly 48.
All inputs are finite; a program needn't handle non-finite values.
Results may differ from a plain program's by a relative error of at most 0.011.
Values may be sent and summed in bfloat16 or wider, within the bound.
No kernel may reach another device: no remote copies, remote signals or barrier semaphores. Data moves between devices by JAX's collectives and lax.ppermute only.
A program may use at most 128 MiB of HBM per device.

v0:
```python
import jax
import jax.numpy as jnp
from jax import lax
from jax.sharding import Mesh
from jax.sharding import PartitionSpec as P

HEADS = 20
HEAD = 64
WIN = 100
GRP = ("grp_0", "grp_1")
LN_EPSILON = 1e-05
RMS_EPSILON = 1e-06
MASKED = -1e30


def extended(cells, sides, width):
    for axis, dim in sides:
        count = lax.axis_size(axis)
        ends = count - 1
        head = lax.slice_in_dim(cells, 0, width, axis=dim)
        tail = lax.slice_in_dim(cells, cells.shape[dim] - width, cells.shape[dim], axis=dim)
        cells = jnp.concatenate(
            [
                lax.ppermute(tail, axis, [(i, (i + 1) % count) for i in range(ends)]),
                cells,
                lax.ppermute(head, axis, [((i + 1) % count, i) for i in range(ends)]),
            ],
            axis=dim,
        )
    return cells


def gather_axes(value, axes, dim):
    out = value
    for number in range(len(axes) - 1, -1, -1):
        out = lax.all_gather(out, axes[number], axis=dim, tiled=True)
    return out


def layer_norm(signal, gain):
    widened = signal.astype(jnp.float32)
    average = jnp.mean(widened, axis=-1, keepdims=True)
    centred = widened - average
    variance = jnp.mean(centred * centred, axis=-1, keepdims=True)
    return centred * lax.rsqrt(variance + LN_EPSILON) * gain


def rms_norm(signal, gain):
    widened = signal.astype(jnp.float32)
    squares = jnp.mean(widened * widened, axis=-1, keepdims=True)
    return widened * lax.rsqrt(squares + RMS_EPSILON) * gain


def body(
    audio,
    block_ids,
    norm_gain,
    qkv_weight,
    out_weight,
    adapter_weight,
    moe_gain,
    gate_weight,
    up_weight,
    down_weight,
    routes,
    route_weights,
):
    frames = audio.shape[1]
    width = audio.shape[2]
    margin = WIN - 1
    signal = audio[0]
    normed = layer_norm(signal, norm_gain).astype(jnp.bfloat16)
    qkv_all = jnp.dot(
        normed,
        lax.all_gather(qkv_weight, GRP, axis=1, tiled=True),
        preferred_element_type=jnp.float32,
    ).astype(jnp.bfloat16)
    tags = (block_ids[0] % 256 + 1).astype(jnp.float32).astype(jnp.bfloat16)
    key_value = qkv_all[:, width:]
    padded_pairs, padded_tags = (
        extended(key_value, (("seq", 0),), margin),
        extended(tags, (("seq", 0),), margin),
    )
    query_rows = qkv_all[:, :width].reshape(frames, HEADS, HEAD)
    key_rows = padded_pairs[:, :width].reshape(-1, HEADS, HEAD)
    value_rows = padded_pairs[:, width:].reshape(-1, HEADS, HEAD)
    scores = jnp.einsum(
        "qhd,khd->hqk", query_rows, key_rows, preferred_element_type=jnp.float32
    ) * HEAD ** (-0.5)
    query_tags = tags.astype(jnp.float32)
    key_tags = padded_tags.astype(jnp.float32)
    distance = (
        jnp.arange(frames, dtype=jnp.int32)[:, None]
        + margin
        - jnp.arange(frames + 2 * margin, dtype=jnp.int32)[None, :]
    )
    allowed = (query_tags[:, None] == key_tags[None, :]) & (jnp.abs(distance) < WIN)
    scores = jnp.where(allowed[None], scores, MASKED)
    highest = jnp.max(scores, axis=-1, keepdims=True)
    exponent = jnp.exp(scores - highest)
    probability = (exponent / jnp.sum(exponent, axis=-1, keepdims=True)).astype(jnp.bfloat16)
    attended = jnp.einsum(
        "hqk,khd->qhd", probability, value_rows, preferred_element_type=jnp.float32
    )
    attended = attended.astype(jnp.bfloat16).reshape(frames, width)
    projected = jnp.dot(
        attended, gather_axes(out_weight, GRP, 1), preferred_element_type=jnp.float32
    )
    encoded = (signal.astype(jnp.float32) + projected).astype(jnp.bfloat16)
    pooled = encoded.reshape(frames // 2, 2 * width)
    thinker_in = jnp.dot(
        pooled,
        lax.all_gather(adapter_weight, GRP, axis=1, tiled=True),
        preferred_element_type=jnp.float32,
    ).astype(jnp.bfloat16)
    expert_in = rms_norm(thinker_in, moe_gain).astype(jnp.bfloat16)
    local_experts = gate_weight.shape[0]
    experts_total = local_experts * lax.axis_size("seq")
    picked_routes = routes[0]
    tokens_here, route_count = picked_routes.shape
    capacity = 3 * tokens_here * route_count // (2 * experts_total)
    chosen_experts = picked_routes.reshape(-1)
    expert_ids = jnp.arange(experts_total, dtype=jnp.int32)
    membership = (chosen_experts[:, None] == expert_ids[None, :]).astype(jnp.int32)
    positions = jnp.sum((jnp.cumsum(membership, axis=0) - 1) * membership, axis=1)
    slot_index = chosen_experts * capacity + positions
    slot_grid = slot_index.reshape(tokens_here, route_count)
    slot_ids = jnp.arange(experts_total * capacity, dtype=jnp.int32)
    dispatch_matrix = jnp.any(slot_grid[None, :, :] == slot_ids[:, None, None], axis=2).astype(
        jnp.bfloat16
    )
    outgoing = jnp.dot(dispatch_matrix, expert_in, preferred_element_type=jnp.float32).astype(
        jnp.bfloat16
    )
    outgoing = outgoing.reshape(experts_total, capacity, expert_in.shape[1])
    arrived = lax.all_to_all(outgoing, "seq", split_axis=0, concat_axis=0, tiled=True)
    senders = arrived.shape[0] // local_experts
    grouped = arrived.reshape(senders, local_experts, arrived.shape[1], arrived.shape[2])
    gate_act = jnp.einsum(
        "secd,edf->secf", grouped, gate_weight, preferred_element_type=jnp.float32
    )
    up_act = jnp.einsum("secd,edf->secf", grouped, up_weight, preferred_element_type=jnp.float32)
    hidden = (jax.nn.silu(gate_act) * up_act).astype(jnp.bfloat16)
    produced = jnp.einsum("secf,efd->secd", hidden, down_weight, preferred_element_type=jnp.float32)
    produced = produced.astype(jnp.bfloat16).reshape(arrived.shape)
    returned = lax.all_to_all(produced, "seq", split_axis=0, concat_axis=0, tiled=True)
    flat_returned = returned.reshape(experts_total * capacity, returned.shape[2])
    picked_rows = (
        flat_returned[slot_index].astype(jnp.float32).reshape(tokens_here, route_count, -1)
    )
    weights_here = route_weights[0]
    shares = weights_here / jnp.sum(weights_here, axis=1, keepdims=True)
    combined = jnp.sum(shares[:, :, None] * picked_rows, axis=1)
    thinker_out = (thinker_in.astype(jnp.float32) + combined).astype(jnp.bfloat16)
    return thinker_out[None]


def solution(mesh):
    torus = Mesh(mesh.devices.reshape(4, 4, mesh.shape["seq"]), ("grp_0", "grp_1", "seq"))
    in_specs = (
        P(GRP, "seq", None),
        P(GRP, "seq"),
        P(),
        P(None, GRP),
        P(None, GRP),
        P(None, GRP),
        P(),
        P("seq", None, None),
        P("seq", None, None),
        P("seq", None, None),
        P(GRP, "seq", None),
        P(GRP, "seq", None),
    )
    out_specs = P(GRP, "seq", None)
    return jax.shard_map(body, mesh=torus, in_specs=in_specs, out_specs=out_specs, check_vma=False)
```

profile of v0, /device:TPU:1, one launch (start us, length us, event | category | flops | bytes accessed | tf_op | source)
XLA Modules:
  0.0 440.4 jit_solution(11311125937926482085)
XLA Ops:
  6.5 0.7 all-gather.4.cloned.1.call-update
  7.3 14.3 %all_gather.13 = bf16[1280,320]{0,1:T(8,128)(2,1)} all-gather(bf16[1280,80]{0,1:T(8,128)(2,1)} %param.16), channel_id=1, replica_groups=mesh['grp_0'=4,'grp_1'=4,'seq'=16] {'grp_1'}, dimensions={1}, use_global_device_ids=true | all-gather | bytes 1024000 | tf_op jit(solution)/shard_map/all_gather | solution.py:36
  21.7 0.7 all-gather.8.cloned.1.call-update
  22.4 0.7 fusion.57
  23.2 6.9 %collective-permute-start.2 = (bf16[99]{0:T(256)(128)(2,1)S(1)}, bf16[99]{0:T(256)(128)(2,1)S(1)}, u32[]{:S(2)}, u32[]{:S(2)}) collective-permute-start(bf16[99]{0:T(256)(128)(2,1)S(1)} %get-tuple-element.13), channel_id=1, source_target_pairs={{0,1},{1,2},{2,3},{3,4},{4,5},{5,6},{6,7},{7,8},{8,9},{9,10},{10,1... | collective-permute-start | bytes 602 | tf_op jit(solution)/shard_map/ppermute | solution.py:24
  30.1 1.9 collective-permute-start.3
  32.0 0.8 copy.30
  32.8 0.1 eq.66
  32.9 0.1 eq.62
  33.0 1.2 reduce-window.6
  34.2 0.2 slice_reduce_fusion
  34.5 0.1 reduce_sum.72
  34.7 0.2 fusion.20
  35.0 1.3 convert_reduce_fusion
  36.3 1.4 fusion.27
  37.7 58.1 %all-gather.4.cloned.1.call-done = bf16[1280,3840]{0,1:T(8,128)(2,1)} async-done(((bf16[1280,240]{0,1:T(8,128)(2,1)}), bf16[1280,3840]{0,1:T(8,128)(2,1)}) %all-gather.4.cloned.1.call-update) | async-done | bytes 9830416 | tf_op jit(solution)/shard_map/all_gather | solution.py:75
  95.8 6.8 %convolution_convert_fusion = bf16[256,3840]{1,0:T(8,128)(2,1)S(1)} fusion(bf16[1280,3840]{0,1:T(8,128)(2,1)} %all-gather.4.cloned.1.call-done, bf16[1,256,1280]{2,1,0:T(8,128)(2,1)} %param.12, f32[1280]{0:T(1024)S(1)} %copy-done.8, f32[256]{0:T(256)S(1)} %add_rsqrt_fusion, f32[256]{0:T(256)S(1)} %broadcast_multiply_fusion.1), kind=kOutput, calls=%fused_computation.6 | convolution fusion | flops 2519203840 | bytes 12459008 | tf_op jit(solution)/shard_map/dot_general | solution.py:73
  102.6 1.1 fusion.60
  103.7 3.9 collective-permute-start
  107.6 2.1 collective-permute-start.1
  109.9 0.2 fusion.41
  110.1 1.2 slice.45
  111.3 0.9 slice.48
  112.1 2.2 copy.27
  114.3 4.5 %collective-permute-done.1 = bf16[99,2560]{1,0:T(8,128)(2,1)} collective-permute-done((bf16[99,2560]{1,0:T(8,128)(2,1)}, bf16[99,2560]{1,0:T(8,128)(2,1)}, u32[]{:S(2)}, u32[]{:S(2)}) %collective-permute-start.1) | collective-permute-done | bytes 506912 | tf_op jit(solution)/shard_map/ppermute | solution.py:26
  118.8 2.1 pad_maximum_fusion
  120.9 1.6 fusion.59
  122.5 2.4 copy.28
  124.9 2.4 copy.26
  127.4 8.2 %fusion.62 = (f32[20,256]{1,0:T(8,128)S(1)}, f32[20,256,454]{1,2,0:T(8,128)}) fusion(pred[256,454]{0,1:T(8,128)(4,1)S(1)} %fusion.41, bf16[256,20,64]{0,2,1:T(8,128)(2,1)} %bitcast.120, bf16[454,20,64]{0,2,1:T(8,128)(2,1)} %bitcast.118), kind=kOutput, calls=%fused_computation.95 | convolution fusion | flops 306831808 | bytes 11252224 | tf_op jit(solution)/shard_map/sub | solution.py:100
  135.6 6.1 %fusion.26 = bf16[20,64,256]{2,1,0:T(8,128)(2,1)} fusion(bf16[454,20,64]{0,2,1:T(8,128)(2,1)} %bitcast.119, f32[20,256,454]{1,2,0:T(8,128)} %get-tuple-element.16, f32[20,256]{1,0:T(8,128)S(1)} %get-tuple-element.15), kind=kOutput, calls=%fused_computation.39 | convolution fusion | flops 302510080 | bytes 11136000 | tf_op jit(solution)/shard_map/hqk,khd->qhd/dot_general | solution.py:102
  141.7 4.2 fusion.11
  145.8 2.1 reshape.244
  147.9 86.9 %all-gather.8.cloned.1.call-done = bf16[2560,2048]{1,0:T(8,128)(2,1)} async-done(((bf16[2560,128]{1,0:T(8,128)(2,1)}), bf16[2560,2048]{1,0:T(8,128)(2,1)}) %all-gather.8.cloned.1.call-update) | async-done | bytes 10485776 | tf_op jit(solution)/shard_map/all_gather | solution.py:113
  234.8 5.8 %multiply_reduce_fusion.1 = (f32[128]{0:T(128)S(1)}, f32[128,2048]{1,0:T(8,128)S(1)}) fusion(bf16[128,2560]{1,0:T(8,128)(2,1)} %reshape.244, bf16[2560,2048]{1,0:T(8,128)(2,1)} %all-gather.8.cloned.1.call-done), kind=kOutput, calls=%fused_computation.45 | convolution fusion | flops 1343225728 | bytes 12190208 | tf_op jit(solution)/shard_map/dot_general | solution.py:111
  240.6 1.1 convolution_convert_fusion.2
  241.7 82.5 %all_to_all.10 = bf16[16,48,2048]{2,1,0:T(8,128)(2,1)S(1)} all-to-all(bf16[16,48,2048]{2,1,0:T(8,128)(2,1)S(1)} %bitcast.117), channel_id=1, replica_groups=mesh['grp_0'=4,'grp_1'=4,'seq'=16] {'seq'}, dimensions={0} | all-to-all | bytes 6291456 | tf_op jit(solution)/shard_map/all_to_all | solution.py:136
  324.2 1.7 copy-done.3
  325.9 4.1 fusion.9
  330.0 10.9 %convolution_convert_fusion.1 = bf16[16,48,2048]{2,1,0:T(8,128)(2,1)} fusion(bf16[1,768,2048]{2,1,0:T(8,128)(2,1)S(1)} %copy-done, bf16[16,48,2048]{2,1,0:T(8,128)(2,1)} %copy-done.3, bf16[1,2048,768]{2,1,0:T(8,128)(2,1)} %param.20, f32[16,48,768]{2,1,0:T(8,128)} %fusion.9), kind=kOutput, calls=%fused_computation.12 | convolution fusion | flops 4836950016 | bytes 14942208 | tf_op jit(solution)/shard_map/secf,efd->secd/dot_general | solution.py:144
  340.9 4.8 %all-to-all-start.1 = ((bf16[16,48,2048]{2,1,0:T(8,128)(2,1)}), bf16[16,48,2048]{2,1,0:T(8,128)(2,1)}, u32[]{:S(2)}, u32[]{:S(2)}) async-start(bf16[16,48,2048]{2,1,0:T(8,128)(2,1)} %convolution_convert_fusion.1), calls=%async_computation.1 | async-start | bytes 6291456 | tf_op jit(solution)/shard_map/all_to_all | solution.py:146
  345.7 0.1 mul.97
  345.8 0.1 copy.29
  346.0 69.2 %all-to-all-done.1 = bf16[16,48,2048]{2,1,0:T(8,128)(2,1)} async-done(((bf16[16,48,2048]{2,1,0:T(8,128)(2,1)}), bf16[16,48,2048]{2,1,0:T(8,128)(2,1)}, u32[]{:S(2)}, u32[]{:S(2)}) %all-to-all-start.1) | async-done | bytes 3145760 | tf_op jit(solution)/shard_map/all_to_all | solution.py:146
  415.1 7.5 %gather_fusion = bf16[512,2048]{1,0:T(8,128)(2,1)} fusion(bf16[768,2048]{1,0:T(8,128)(2,1)} %bitcast.26, s32[1024]{0:T(1024)S(1)} %pad_clamp_fusion), kind=kCustom, calls=%fused_computation | custom fusion | bytes 4196352 | tf_op jit(solution)/shard_map/gather | solution.py:149
  422.7 4.8 %reshape.252 = f32[128,4,2048]{2,1,0:T(4,128)} reshape(bf16[512,2048]{1,0:T(8,128)(2,1)} %gather_fusion) | data formatting | bytes 6291456 | tf_op jit(solution)/shard_map/convert_element_type | solution.py:149
  427.4 5.5 %multiply_reduce_fusion = f32[128,2048]{1,0:T(8,128)S(1)} fusion(f32[128,4,2048]{2,1,0:T(4,128)} %reshape.252, f32[128,4]{1,0:T(8,128)S(1)} %copy.29), kind=kLoop, calls=%fused_computation.11 | loop fusion | flops 1835008 | bytes 5244928 | tf_op jit(solution)/shard_map/reduce_sum | solution.py:153
  433.0 0.9 fusion.38
  (42 shorter events, 0.6 us)
Async XLA Ops:
  6.5 323.5 %copy-start = (bf16[1,768,2048]{2,1,0:T(8,128)(2,1)S(1)}, bf16[1,768,2048]{2,1,0:T(8,128)(2,1)}, u32[]{:S(2)}) copy-start(bf16[1,768,2048]{2,1,0:T(8,128)(2,1)} %param.21) | copy-start | bytes 9437188
  6.5 89.2 %copy-start.8 = (f32[1280]{0:T(1024)S(1)}, f32[1280]{0:T(1024)}, u32[]{:S(2)}) copy-start(f32[1280]{0:T(1024)} %param.14) | copy-start | bytes 15364
  6.5 89.2 %all-gather.4.cloned.1.call-start = ((), (), s32[]{:S(2)}) async-start(), calls=%async_computation.2 | async-start | bytes 10444800 | tf_op jit(solution)/shard_map/all_gather | solution.py:75
  7.3 134.4 %all-gather.6.cloned.1.call-start = ((), (), s32[]{:S(2)}) async-start(), calls=%async_computation.3 | async-start | bytes 4096000 | tf_op jit(solution)/shard_map/all_gather | solution.py:36
  21.7 213.1 %all-gather.8.cloned.1.call-start = ((), (), s32[]{:S(2)}) async-start(), calls=%async_computation.4 | async-start | bytes 11141120 | tf_op jit(solution)/shard_map/all_gather | solution.py:113
  23.2 86.6 %collective-permute-start.2 = (bf16[99]{0:T(256)(128)(2,1)S(1)}, bf16[99]{0:T(256)(128)(2,1)S(1)}, u32[]{:S(2)}, u32[]{:S(2)}) collective-permute-start(bf16[99]{0:T(256)(128)(2,1)S(1)} %get-tuple-element.13), channel_id=1, source_target_pairs={{0,1},{1,2},{2,3},{3,4},{4,5},{5,6},{6,7},{7,8},{8,9},{9,10},{10,1... | collective-permute-start | bytes 602 | tf_op jit(solution)/shard_map/ppermute | solution.py:24
  30.1 79.7 %collective-permute-start.3 = (bf16[99]{0:T(256)(128)(2,1)S(1)}, bf16[99]{0:T(256)(128)(2,1)S(1)}, u32[]{:S(2)}, u32[]{:S(2)}) collective-permute-start(bf16[99]{0:T(256)(128)(2,1)S(1)} %get-tuple-element.14), channel_id=1, source_target_pairs={{1,0},{2,1},{3,2},{4,3},{5,4},{6,5},{7,6},{8,7},{9,8},{10,9},{11,1... | collective-permute-start | bytes 602 | tf_op jit(solution)/shard_map/ppermute | solution.py:26
  37.7 72.1 %copy-start.6 = (s32[1,256]{1,0:T(1,128)S(1)}, s32[1,256]{1,0:T(1,128)}, u32[]{:S(2)}) copy-start(s32[1,256]{1,0:T(1,128)} %param.13) | copy-start | bytes 3076
  103.7 10.6 %collective-permute-start = (bf16[99,2560]{1,0:T(8,128)(2,1)}, bf16[99,2560]{1,0:T(8,128)(2,1)}, u32[]{:S(2)}, u32[]{:S(2)}) collective-permute-start(bf16[99,2560]{1,0:T(8,128)(2,1)} %get-tuple-element.9), channel_id=1, source_target_pairs={{0,1},{1,2},{2,3},{3,4},{4,5},{5,6},{6,7},{7,8},{8,9},{9,10},{10,1... | collective-permute-start | bytes 1520648 | tf_op jit(solution)/shard_map/ppermute | solution.py:24
  107.6 11.2 %collective-permute-start.1 = (bf16[99,2560]{1,0:T(8,128)(2,1)}, bf16[99,2560]{1,0:T(8,128)(2,1)}, u32[]{:S(2)}, u32[]{:S(2)}) collective-permute-start(bf16[99,2560]{1,0:T(8,128)(2,1)} %get-tuple-element.10), channel_id=1, source_target_pairs={{1,0},{2,1},{3,2},{4,3},{5,4},{6,5},{7,6},{8,7},{9,8},{10,9},{11,1... | collective-permute-start | bytes 1520648 | tf_op jit(solution)/shard_map/ppermute | solution.py:26
  147.9 92.7 %copy-start.4 = (f32[2048]{0:T(1024)S(1)}, f32[2048]{0:T(1024)}, u32[]{:S(2)}) copy-start(f32[2048]{0:T(1024)} %param.18) | copy-start | bytes 24580
  240.6 83.6 %copy-start.1 = (f32[128,2048]{1,0:T(8,128)}, f32[128,2048]{1,0:T(8,128)S(1)}, u32[]{:S(2)}) copy-start(f32[128,2048]{1,0:T(8,128)S(1)} %get-tuple-element.18) | copy-start | bytes 3145732
  241.7 84.2 %copy-start.7 = (bf16[1,2048,768]{2,1,0:T(8,128)(2,1)S(1)}, bf16[1,2048,768]{2,1,0:T(8,128)(2,1)}, u32[]{:S(2)}) copy-start(bf16[1,2048,768]{2,1,0:T(8,128)(2,1)} %param.19) | copy-start | bytes 9437188
  324.2 1.7 copy-start.3
  340.9 4.9 %copy-start.5 = (f32[1,128,4]{1,2,0:T(4,128)S(1)}, f32[1,128,4]{1,2,0:T(4,128)}, u32[]{:S(2)}) copy-start(f32[1,128,4]{1,2,0:T(4,128)} %param.23) | copy-start | bytes 6148
  340.9 74.2 %all-to-all-start.1 = ((bf16[16,48,2048]{2,1,0:T(8,128)(2,1)}), bf16[16,48,2048]{2,1,0:T(8,128)(2,1)}, u32[]{:S(2)}, u32[]{:S(2)}) async-start(bf16[16,48,2048]{2,1,0:T(8,128)(2,1)} %convolution_convert_fusion.1), calls=%async_computation.1 | async-start | bytes 6291456 | tf_op jit(solution)/shard_map/all_to_all | solution.py:146
  427.4 5.5 %copy-start.2 = (f32[128,2048]{1,0:T(8,128)S(1)}, f32[128,2048]{1,0:T(8,128)}, u32[]{:S(2)}) copy-start(f32[128,2048]{1,0:T(8,128)} %copy-done.1) | copy-start | bytes 3145732
Sparse Core Ops, SparseCore 0:
  9.8 85.9 all-gather.3
  97.6 42.8 all-gather.5
  142.9 91.8 all-gather.7
where the time goes:
time: 441 us; the launch traced here: 440 us
  waiting for transfers between devices  220 us (50%)
  blocking collectives  96.8 us (22%)
  matrix products  47.2 us (11%)
  local copies, waits for them, and re-layouts  29.6 us (7%)
  starting transfers between devices  19.7 us (4%)
  other arithmetic  13.7 us (3%)
  between operations  13.4 us (3%)
    all_gather x1, waiting for transfers between devices, body(): lax.all_gather(adapter_weight, GRP, axis=1, tiled=True)  86.9 us
    all_to_all x1, blocking collectives, body(): lax.all_to_all(outgoing, 'seq', split_axis=0, concat_axis=0, tiled=True)  82.5 us
    all_to_all x1, waiting for transfers between devices, body(): lax.all_to_all(produced, 'seq', split_axis=0, concat_axis=0, tiled=True)  69.2 us
    all_gather x1, waiting for transfers between devices, body(): lax.all_gather(qkv_weight, GRP, axis=1, tiled=True)  58.1 us
    all_gather x1, blocking collectives, gather_axes(): out = lax.all_gather(out, axes[number], axis=dim, tiled=True)  14.3 us
    dot_general x1, matrix products, body(): jnp.einsum('secf,efd->secd', hidden, down_weight, preferred_element_type=...  10.9 us
    ppermute x2, starting transfers between devices, extended(): lax.ppermute(tail, axis, [(i, (i + 1) % count) for i in range(ends)])  10.8 us
  transfers between devices with their start and end apart: 8, of which 4 were waited for; matrix products, arithmetic and copies ran while one was open for 11% of the time, Pallas kernels for 0%

commit v1 on v0

--- a/solution.py
+++ b/solution.py
@@ -72,7 +72,9 @@
     normed = layer_norm(signal, norm_gain).astype(jnp.bfloat16)
     qkv_all = jnp.dot(
         normed,
-        lax.all_gather(qkv_weight, GRP, axis=1, tiled=True),
+        jnp.concatenate(
+            lax.all_to_all(jnp.stack([qkv_weight] * lax.axis_size(GRP)), GRP, 0, 0), axis=1
+        ),
         preferred_element_type=jnp.float32,
     ).astype(jnp.bfloat16)
     tags = (block_ids[0] % 256 + 1).astype(jnp.float32).astype(jnp.bfloat16)

time: 441 us -> 479 us (1.086)
  waiting for transfers between devices: 220 us -> 243 us
  starting transfers between devices: 19.7 us -> 29.7 us
    all_to_all x0 -> x1, waiting for transfers between devices: none -> 123 us  [body(): lax.all_to_all(jnp.stack([qkv_weight] * lax.axis_size(GRP)), GRP, 0, 0)]
    all_gather x1 -> x0, waiting for transfers between devices: 58.1 us -> none  [body(): lax.all_gather(qkv_weight, GRP, axis=1, tiled=True)]
    all_gather x1, waiting for transfers between devices: 86.9 us -> 48.3 us  [body(): lax.all_gather(adapter_weight, GRP, axis=1, tiled=True)]
    ppermute x2, starting transfers between devices: 4.02 us -> 12.4 us  [extended(): lax.ppermute(head, axis, [((i + 1) % count, i) for i in range(ends)])]
    another operation x1 -> x2, local copies, waits for them, and re-layouts: 0.01 us -> 5.44 us  [the longest x1 5.43 us: body(): jnp.stack([qkv_weight] * lax.axis_size(GRP))]
    all_to_all x0 -> x1, starting transfers between devices: none -> 5.38 us  [body(): lax.all_to_all(jnp.stack([qkv_weight] * lax.axis_size(GRP)), GRP, 0, 0)]
  transfers between devices with their start and end apart: 8 -> 8, of which waited for: 4 -> 5; matrix products, arithmetic and copies ran while one was open for 11% -> 11% of each run, Pallas kernels for 0% -> 0%
where the time goes in v1:
time: 479 us; the launch traced here: 478 us
  waiting for transfers between devices  243 us (51%)
  blocking collectives  97 us (20%)
  matrix products  47.1 us (10%)
  local copies, waits for them, and re-layouts  34.3 us (7%)
  starting transfers between devices  29.7 us (6%)
  between operations  13.7 us (3%)
  other arithmetic  13.1 us (3%)
    all_to_all x1, waiting for transfers between devices, body(): lax.all_to_all(jnp.stack([qkv_weight] * lax.axis_size(GRP)), GRP, 0, 0)  123 us
    all_to_all x1, blocking collectives, body(): lax.all_to_all(outgoing, 'seq', split_axis=0, concat_axis=0, tiled=True)  82.5 us
    all_to_all x1, waiting for transfers between devices, body(): lax.all_to_all(produced, 'seq', split_axis=0, concat_axis=0, tiled=True)  69.2 us
    all_gather x1, waiting for transfers between devices, body(): lax.all_gather(adapter_weight, GRP, axis=1, tiled=True)  48.3 us
    all_gather x1, blocking collectives, gather_axes(): out = lax.all_gather(out, axes[number], axis=dim, tiled=True)  14.5 us
    ppermute x2, starting transfers between devices, extended(): lax.ppermute(head, axis, [((i + 1) % count, i) for i in range(ends)])  12.4 us
    dot_general x1, matrix products, body(): jnp.einsum('secf,efd->secd', hidden, down_weight, preferred_element_type=...  11 us
  transfers between devices with their start and end apart: 8, of which 5 were waited for; matrix products, arithmetic and copies ran while one was open for 11% of the time, Pallas kernels for 0%

profile of v1, /device:TPU:1, one launch (start us, length us, event | category | flops | bytes accessed | tf_op | source)
XLA Modules:
  0.0 478.1 jit_solution(8492060302653065535)
XLA Ops:
  6.5 14.5 %all_gather.9 = bf16[1280,320]{0,1:T(8,128)(2,1)} all-gather(bf16[1280,80]{0,1:T(8,128)(2,1)} %param.16), channel_id=1, replica_groups=mesh['grp_0'=4,'grp_1'=4,'seq'=16] {'grp_1'}, dimensions={1}, use_global_device_ids=true | all-gather | bytes 1024000 | tf_op jit(solution)/shard_map/all_gather | solution.py:36
  21.1 0.7 all-gather.5.cloned.1.call-update
  21.8 5.4 %stack.2 = bf16[16,1280,240]{1,2,0:T(8,128)(2,1)} broadcast(bf16[1280,240]{0,1:T(8,128)(2,1)} %param.15), dimensions={1,2} | broadcast | bytes 10444800 | tf_op jit(solution)/shard_map/stack | solution.py:76
  27.3 5.4 %all-to-all-start = ((bf16[16,1280,240]{1,2,0:T(8,128)(2,1)}), bf16[16,1280,240]{1,2,0:T(8,128)(2,1)}, u32[]{:S(2)}, u32[]{:S(2)}) async-start(bf16[16,1280,240]{1,2,0:T(8,128)(2,1)} %stack.2), calls=%async_computation | async-start | bytes 19660800 | tf_op jit(solution)/shard_map/all_to_all | solution.py:76
  32.7 5.8 %collective-permute-start.3 = (bf16[99]{0:T(256)(128)(2,1)S(1)}, bf16[99]{0:T(256)(128)(2,1)S(1)}, u32[]{:S(2)}, u32[]{:S(2)}) collective-permute-start(bf16[99]{0:T(256)(128)(2,1)S(1)} %get-tuple-element.14), channel_id=1, source_target_pairs={{1,0},{2,1},{3,2},{4,3},{5,4},{6,5},{7,6},{8,7},{9,8},{10,9},{11,1... | collective-permute-start | bytes 602 | tf_op jit(solution)/shard_map/ppermute | solution.py:26
  38.6 3.4 collective-permute-start.2
  42.0 0.1 copy.31
  42.1 0.1 eq.62
  42.2 0.1 eq.66
  42.4 1.2 reduce-window.6
  43.5 0.2 slice_reduce_fusion
  43.9 0.1 reduce_sum.72
  44.1 0.2 fusion.20
  44.3 1.3 convert_reduce_fusion
  45.6 1.4 fusion.26
  47.0 123.3 %all-to-all-done = bf16[16,1280,240]{1,2,0:T(8,128)(2,1)} async-done(((bf16[16,1280,240]{1,2,0:T(8,128)(2,1)}), bf16[16,1280,240]{1,2,0:T(8,128)(2,1)}, u32[]{:S(2)}, u32[]{:S(2)}) %all-to-all-start) | async-done | bytes 9830432 | tf_op jit(solution)/shard_map/all_to_all | solution.py:76
  170.3 6.8 %convolution_convert_fusion = bf16[256,3840]{1,0:T(8,128)(2,1)S(1)} fusion(bf16[1280,3840]{0,1:T(8,128)(2,1)} %bitcast.3, bf16[1,256,1280]{2,1,0:T(8,128)(2,1)} %param.12, f32[1280]{0:T(1024)S(1)} %copy-done.9, f32[256]{0:T(256)S(1)} %add_rsqrt_fusion, f32[256]{0:T(256)S(1)} %broadcast_multiply_fusion.1), kind=kOutput, calls=%fused_computation.6 | convolution fusion | flops 2519203840 | bytes 12459008 | tf_op jit(solution)/shard_map/dot_general | solution.py:73
  177.1 1.1 fusion.61
  178.2 6.6 %collective-permute-start.1 = (bf16[99,2560]{1,0:T(8,128)(2,1)}, bf16[99,2560]{1,0:T(8,128)(2,1)}, u32[]{:S(2)}, u32[]{:S(2)}) collective-permute-start(bf16[99,2560]{1,0:T(8,128)(2,1)} %get-tuple-element.10), channel_id=1, source_target_pairs={{1,0},{2,1},{3,2},{4,3},{5,4},{6,5},{7,6},{8,7},{9,8},{10,9},{11,1... | collective-permute-start | bytes 1520648 | tf_op jit(solution)/shard_map/ppermute | solution.py:26
  184.9 3.6 collective-permute-start
  188.6 0.2 fusion.42
  188.8 1.2 slice.45
  190.0 0.9 slice.48
  190.8 2.2 copy.28
  193.0 0.6 collective-permute-done.1
  193.6 1.2 collective-permute-done
  194.8 2.1 pad_maximum_fusion
  197.0 1.6 fusion.60
  198.5 2.4 copy.27
  200.9 2.4 copy.29
  203.3 8.2 %fusion.63 = (f32[20,256]{1,0:T(8,128)S(1)}, f32[20,256,454]{1,2,0:T(8,128)}) fusion(pred[256,454]{0,1:T(8,128)(4,1)S(1)} %fusion.42, bf16[256,20,64]{0,2,1:T(8,128)(2,1)} %bitcast.119, bf16[454,20,64]{0,2,1:T(8,128)(2,1)} %bitcast.118), kind=kOutput, calls=%fused_computation.97 | convolution fusion | flops 306831808 | bytes 11252224 | tf_op jit(solution)/shard_map/sub | solution.py:102
  211.5 6.0 %fusion.24 = bf16[20,64,256]{2,1,0:T(8,128)(2,1)} fusion(bf16[454,20,64]{0,2,1:T(8,128)(2,1)} %bitcast.117, f32[20,256,454]{1,2,0:T(8,128)} %get-tuple-element.16, f32[20,256]{1,0:T(8,128)S(1)} %get-tuple-element.15), kind=kOutput, calls=%fused_computation.38 | convolution fusion | flops 302510080 | bytes 11136000 | tf_op jit(solution)/shard_map/hqk,khd->qhd/dot_general | solution.py:104
  217.6 4.2 fusion.11
  221.8 2.1 reshape.275
  223.9 48.3 %all-gather.5.cloned.1.call-done = bf16[2560,2048]{1,0:T(8,128)(2,1)} async-done(((bf16[2560,128]{1,0:T(8,128)(2,1)}), bf16[2560,2048]{1,0:T(8,128)(2,1)}) %all-gather.5.cloned.1.call-update) | async-done | bytes 10485776 | tf_op jit(solution)/shard_map/all_gather | solution.py:115
  272.2 5.8 %multiply_reduce_fusion.1 = (f32[128]{0:T(128)S(1)}, f32[128,2048]{1,0:T(8,128)S(1)}) fusion(bf16[128,2560]{1,0:T(8,128)(2,1)} %reshape.275, bf16[2560,2048]{1,0:T(8,128)(2,1)} %all-gather.5.cloned.1.call-done), kind=kOutput, calls=%fused_computation.46 | convolution fusion | flops 1343225728 | bytes 12190208 | tf_op jit(solution)/shard_map/dot_general | solution.py:113
  278.0 1.1 convolution_convert_fusion.2
  279.1 82.5 %all_to_all.15 = bf16[16,48,2048]{2,1,0:T(8,128)(2,1)S(1)} all-to-all(bf16[16,48,2048]{2,1,0:T(8,128)(2,1)S(1)} %bitcast.116), channel_id=1, replica_groups=mesh['grp_0'=4,'grp_1'=4,'seq'=16] {'seq'}, dimensions={0} | all-to-all | bytes 6291456 | tf_op jit(solution)/shard_map/all_to_all | solution.py:138
  361.6 1.7 copy-done.3
  363.3 4.0 fusion.9
  367.3 11.0 %convolution_convert_fusion.1 = bf16[16,48,2048]{2,1,0:T(8,128)(2,1)} fusion(bf16[1,768,2048]{2,1,0:T(8,128)(2,1)S(1)} %copy-done, bf16[16,48,2048]{2,1,0:T(8,128)(2,1)} %copy-done.3, bf16[1,2048,768]{2,1,0:T(8,128)(2,1)} %param.20, f32[16,48,768]{2,1,0:T(8,128)} %fusion.9), kind=kOutput, calls=%fused_computation.12 | convolution fusion | flops 4836950016 | bytes 14942208 | tf_op jit(solution)/shard_map/secf,efd->secd/dot_general | solution.py:146
  378.3 4.8 all-to-all-start.2
  383.2 0.1 copy.30
  383.4 69.2 %all-to-all-done.2 = bf16[16,48,2048]{2,1,0:T(8,128)(2,1)} async-done(((bf16[16,48,2048]{2,1,0:T(8,128)(2,1)}), bf16[16,48,2048]{2,1,0:T(8,128)(2,1)}, u32[]{:S(2)}, u32[]{:S(2)}) %all-to-all-start.2) | async-done | bytes 3145760 | tf_op jit(solution)/shard_map/all_to_all | solution.py:148
  452.6 7.5 %gather_fusion = bf16[512,2048]{1,0:T(8,128)(2,1)} fusion(bf16[768,2048]{1,0:T(8,128)(2,1)} %bitcast.29, s32[1024]{0:T(1024)S(1)} %pad_clamp_fusion), kind=kCustom, calls=%fused_computation | custom fusion | bytes 4196352 | tf_op jit(solution)/shard_map/gather | solution.py:151
  460.1 4.8 reshape.283
  464.8 5.5 %multiply_reduce_fusion = f32[128,2048]{1,0:T(8,128)S(1)} fusion(f32[128,4,2048]{2,1,0:T(4,128)} %reshape.283, f32[128,4]{1,0:T(8,128)S(1)} %copy.30), kind=kLoop, calls=%fused_computation.11 | loop fusion | flops 1835008 | bytes 5244928 | tf_op jit(solution)/shard_map/reduce_sum | solution.py:155
  470.3 0.9 fusion.39
  (44 shorter events, 0.7 us)
Async XLA Ops:
  6.5 360.8 %copy-start = (bf16[1,768,2048]{2,1,0:T(8,128)(2,1)S(1)}, bf16[1,768,2048]{2,1,0:T(8,128)(2,1)}, u32[]{:S(2)}) copy-start(bf16[1,768,2048]{2,1,0:T(8,128)(2,1)} %param.21) | copy-start | bytes 9437188
  6.5 211.0 %all-gather.3.cloned.1.call-start = ((), (), s32[]{:S(2)}) async-start(), calls=%async_computation.3 | async-start | bytes 4096000 | tf_op jit(solution)/shard_map/all_gather | solution.py:36
  21.1 251.1 %all-gather.5.cloned.1.call-start = ((), (), s32[]{:S(2)}) async-start(), calls=%async_computation.4 | async-start | bytes 11141120 | tf_op jit(solution)/shard_map/all_gather | solution.py:115
  27.2 5.4 %copy-start.7 = (s32[1,256]{1,0:T(1,128)S(1)}, s32[1,256]{1,0:T(1,128)}, u32[]{:S(2)}) copy-start(s32[1,256]{1,0:T(1,128)} %param.13) | copy-start | bytes 3076
  27.2 14.8 %copy-start.6 = (s32[1,128,4]{1,2,0:T(4,128)S(1)}, s32[1,128,4]{1,2,0:T(4,128)}, u32[]{:S(2)}) copy-start(s32[1,128,4]{1,2,0:T(4,128)} %param.22) | copy-start | bytes 6148
  27.3 143.0 %copy-start.9 = (f32[1280]{0:T(1024)S(1)}, f32[1280]{0:T(1024)}, u32[]{:S(2)}) copy-start(f32[1280]{0:T(1024)} %param.14) | copy-start | bytes 15364
  27.3 143.0 %all-to-all-start = ((bf16[16,1280,240]{1,2,0:T(8,128)(2,1)}), bf16[16,1280,240]{1,2,0:T(8,128)(2,1)}, u32[]{:S(2)}, u32[]{:S(2)}) async-start(bf16[16,1280,240]{1,2,0:T(8,128)(2,1)} %stack.2), calls=%async_computation | async-start | bytes 19660800 | tf_op jit(solution)/shard_map/all_to_all | solution.py:76
  32.7 155.8 %collective-permute-start.3 = (bf16[99]{0:T(256)(128)(2,1)S(1)}, bf16[99]{0:T(256)(128)(2,1)S(1)}, u32[]{:S(2)}, u32[]{:S(2)}) collective-permute-start(bf16[99]{0:T(256)(128)(2,1)S(1)} %get-tuple-element.14), channel_id=1, source_target_pairs={{1,0},{2,1},{3,2},{4,3},{5,4},{6,5},{7,6},{8,7},{9,8},{10,9},{11,1... | collective-permute-start | bytes 602 | tf_op jit(solution)/shard_map/ppermute | solution.py:26
  38.6 150.0 %collective-permute-start.2 = (bf16[99]{0:T(256)(128)(2,1)S(1)}, bf16[99]{0:T(256)(128)(2,1)S(1)}, u32[]{:S(2)}, u32[]{:S(2)}) collective-permute-start(bf16[99]{0:T(256)(128)(2,1)S(1)} %get-tuple-element.13), channel_id=1, source_target_pairs={{0,1},{1,2},{2,3},{3,4},{4,5},{5,6},{6,7},{7,8},{8,9},{9,10},{10,1... | collective-permute-start | bytes 602 | tf_op jit(solution)/shard_map/ppermute | solution.py:24
  178.2 15.4 %collective-permute-start.1 = (bf16[99,2560]{1,0:T(8,128)(2,1)}, bf16[99,2560]{1,0:T(8,128)(2,1)}, u32[]{:S(2)}, u32[]{:S(2)}) collective-permute-start(bf16[99,2560]{1,0:T(8,128)(2,1)} %get-tuple-element.10), channel_id=1, source_target_pairs={{1,0},{2,1},{3,2},{4,3},{5,4},{6,5},{7,6},{8,7},{9,8},{10,9},{11,1... | collective-permute-start | bytes 1520648 | tf_op jit(solution)/shard_map/ppermute | solution.py:26
  184.9 10.0 %collective-permute-start = (bf16[99,2560]{1,0:T(8,128)(2,1)}, bf16[99,2560]{1,0:T(8,128)(2,1)}, u32[]{:S(2)}, u32[]{:S(2)}) collective-permute-start(bf16[99,2560]{1,0:T(8,128)(2,1)} %get-tuple-element.9), channel_id=1, source_target_pairs={{0,1},{1,2},{2,3},{3,4},{4,5},{5,6},{6,7},{7,8},{8,9},{9,10},{10,1... | collective-permute-start | bytes 1520648 | tf_op jit(solution)/shard_map/ppermute | solution.py:24
  223.8 54.2 %copy-start.4 = (f32[2048]{0:T(1024)S(1)}, f32[2048]{0:T(1024)}, u32[]{:S(2)}) copy-start(f32[2048]{0:T(1024)} %param.18) | copy-start | bytes 24580
  278.0 83.6 %copy-start.1 = (f32[128,2048]{1,0:T(8,128)}, f32[128,2048]{1,0:T(8,128)S(1)}, u32[]{:S(2)}) copy-start(f32[128,2048]{1,0:T(8,128)S(1)} %get-tuple-element.18) | copy-start | bytes 3145732
  279.1 84.2 %copy-start.8 = (bf16[1,2048,768]{2,1,0:T(8,128)(2,1)S(1)}, bf16[1,2048,768]{2,1,0:T(8,128)(2,1)}, u32[]{:S(2)}) copy-start(bf16[1,2048,768]{2,1,0:T(8,128)(2,1)} %param.19) | copy-start | bytes 9437188
  361.6 1.7 copy-start.3
  378.3 4.9 %copy-start.5 = (f32[1,128,4]{1,2,0:T(4,128)S(1)}, f32[1,128,4]{1,2,0:T(4,128)}, u32[]{:S(2)}) copy-start(f32[1,128,4]{1,2,0:T(4,128)} %param.23) | copy-start | bytes 6148
  378.3 74.2 %all-to-all-start.2 = ((bf16[16,48,2048]{2,1,0:T(8,128)(2,1)}), bf16[16,48,2048]{2,1,0:T(8,128)(2,1)}, u32[]{:S(2)}, u32[]{:S(2)}) async-start(bf16[16,48,2048]{2,1,0:T(8,128)(2,1)} %convolution_convert_fusion.1), calls=%async_computation.2 | async-start | bytes 6291456 | tf_op jit(solution)/shard_map/all_to_all | solution.py:148
  464.8 5.5 %copy-start.2 = (f32[128,2048]{1,0:T(8,128)S(1)}, f32[128,2048]{1,0:T(8,128)}, u32[]{:S(2)}) copy-start(f32[128,2048]{1,0:T(8,128)} %copy-done.1) | copy-start | bytes 3145732
Sparse Core Ops, SparseCore 0:
  21.2 145.9 all-gather.2
  169.6 102.5 all-gather.4
